TPU v7x, 32 devices: a whole 2x2x4 slice. The times are simulated.
32 devices in a mesh: dp: 8 (over y, x, core), ctx: 4 (over z).
Axes of the slice: x: 2, y: 2, z: 4, core: 2. Of those that a mesh axis runs over, the one named last changes fastest.
Arguments:
- layer_input: bfloat16 [8, 1024, 1024], P('dp', 'ctx'), may hold values from -6 to 6
- prefix: int32 [8], P('dp'), may hold values from 102 to 512, as said below
- ln1_gain: bfloat16 [1024], P(('dp', 'ctx')), may hold values from 0.5 to 1.5
- ln1_bias: bfloat16 [1024], P(('dp', 'ctx')), may hold values from -3 to 3
- w_qkv: bfloat16 [1024, 3072], P(('dp', 'ctx')), may hold values from -0.1875 to 0.1875
- b_qv: bfloat16 [2048], P(('dp', 'ctx')), may hold values from -4 to 4
- w_out: bfloat16 [1024, 1024], P(('dp', 'ctx')), may hold values from -3 to 3
- b_out: bfloat16 [1024], P(('dp', 'ctx')), may hold values from -3 to 3
- ln2_gain: bfloat16 [1024], P(('dp', 'ctx')), may hold values from 0.5 to 1.5
- ln2_bias: bfloat16 [1024], P(('dp', 'ctx')), may hold values from -3 to 3
- w_up: bfloat16 [1024, 4096], P(('dp', 'ctx')), may hold values from -0.1875 to 0.1875
- b_up: bfloat16 [4096], P(('dp', 'ctx')), may hold values from -4 to 4
- w_down: bfloat16 [4096, 1024], P(('dp', 'ctx')), may hold values from -0.09375 to 0.09375
- b_down: bfloat16 [1024], P(('dp', 'ctx')), may hold values from -6 to 6
- cotangent: bfloat16 [8, 1024, 1024], P('dp', 'ctx'), may hold values from -6 to 6
Outputs:
- layer_out: bfloat16 [8, 1024, 1024], P('dp', 'ctx')
- input_grad: float32 [8, 1024, 1024], P('dp', 'ctx')
- grad_ln1_gain: float32 [1024], P(('dp', 'ctx'))
- grad_ln1_bias: float32 [1024], P(('dp', 'ctx'))
- grad_w_qkv: float32 [1024, 3072], P(('dp', 'ctx'))
- grad_b_qv: float32 [2048], P(('dp', 'ctx'))
- grad_w_out: float32 [1024, 1024], P(('dp', 'ctx'))
- grad_b_out: float32 [1024], P(('dp', 'ctx'))
- grad_ln2_gain: float32 [1024], P(('dp', 'ctx'))
- grad_ln2_bias: float32 [1024], P(('dp', 'ctx'))
- grad_w_up: float32 [1024, 4096], P(('dp', 'ctx'))
- grad_b_up: float32 [4096], P(('dp', 'ctx'))
- grad_w_down: float32 [4096, 1024], P(('dp', 'ctx'))
- grad_b_down: float32 [1024], P(('dp', 'ctx'))
Inputs may be any that keep to these rules, and one draw needn't show every extreme that they name: prefix[s] counts the leading positions of sequence s that attend to one another in both directions; the largest and the smallest allowed values both occur.
All inputs are finite; a program needn't handle non-finite values.
Results may differ from a plain program's by a relative error of at most 0.012.
Values may be sent and summed in bfloat16 or wider, within the bound.
No kernel may reach another device: no remote copies, remote signals or barrier semaphores. Data moves between devices by JAX's collectives and lax.ppermute only.
A program may use at most 192 MiB of HBM per device.

v0:
```python
import jax
import jax.numpy as jnp
from jax import lax
from jax.sharding import PartitionSpec as P

D = 1024
H = 16
HD = 64
NEGATIVE = -1e30


def layer_norm(values, gain, shift):
    center = jnp.mean(values, axis=-1, keepdims=True)
    offsets = values - center
    spread = jnp.mean(offsets * offsets, axis=-1, keepdims=True)
    return offsets * lax.rsqrt(spread + 1e-05) * gain + shift


def gelu_tanh(values):
    return jax.nn.gelu(values, approximate=True)


def masked_scores(query_heads, query_pos, key_heads, key_pos, prefix_len):
    raw_scores = (
        jnp.einsum("qhd,khd->hqk", query_heads, key_heads, preferred_element_type=jnp.float32)
        * 0.125
    )
    allowed = (key_pos[None, :] <= query_pos[:, None]) | (key_pos[None, :] < prefix_len)
    return (jnp.where(allowed[None], raw_scores, NEGATIVE), allowed)


def softmax_rows(query_heads, query_pos, key_heads, key_pos, prefix_len, log_total):
    scores, allowed = masked_scores(query_heads, query_pos, key_heads, key_pos, prefix_len)
    return jnp.where(allowed[None], jnp.exp(scores - log_total[:, :, None]), 0.0)


def per_device(
    layer_input,
    prefix,
    ln1_gain,
    ln1_bias,
    w_qkv,
    b_qv,
    w_out,
    b_out,
    ln2_gain,
    ln2_bias,
    w_up,
    b_up,
    w_down,
    b_down,
    cotangent,
):
    (
        gain_first,
        shift_first,
        proj_qkv,
        bias_qv,
        proj_out,
        bias_out,
        gain_second,
        shift_second,
        proj_up,
        bias_up,
        proj_down,
        bias_down,
    ) = (
        lax.all_gather(ln1_gain, ("dp", "ctx"), axis=0, tiled=True),
        lax.all_gather(ln1_bias, ("dp", "ctx"), axis=0, tiled=True),
        lax.all_gather(w_qkv, ("dp", "ctx"), axis=0, tiled=True),
        lax.all_gather(b_qv, ("dp", "ctx"), axis=0, tiled=True),
        lax.all_gather(w_out, ("dp", "ctx"), axis=0, tiled=True),
        lax.all_gather(b_out, ("dp", "ctx"), axis=0, tiled=True),
        lax.all_gather(ln2_gain, ("dp", "ctx"), axis=0, tiled=True),
        lax.all_gather(ln2_bias, ("dp", "ctx"), axis=0, tiled=True),
        lax.all_gather(w_up, ("dp", "ctx"), axis=0, tiled=True),
        lax.all_gather(b_up, ("dp", "ctx"), axis=0, tiled=True),
        lax.all_gather(w_down, ("dp", "ctx"), axis=0, tiled=True),
        lax.all_gather(b_down, ("dp", "ctx"), axis=0, tiled=True),
    )
    tokens = layer_input.shape[1]
    length = tokens * lax.axis_size("ctx")
    block_rows = min(512, length)
    block_count = length // block_rows
    prefix_len = prefix[0]
    query_pos = lax.axis_index("ctx") * tokens + jnp.arange(tokens, dtype=jnp.int32)
    block_starts = jnp.arange(block_count, dtype=jnp.int32) * block_rows
    local_rows = jnp.arange(block_rows, dtype=jnp.int32)
    inputs = layer_input[0].astype(jnp.float32)
    upstream = cotangent[0].astype(jnp.float32)
    shift_one = shift_first.astype(jnp.float32)
    shift_two = shift_second.astype(jnp.float32)
    hidden_first = layer_norm(inputs, gain_first.astype(jnp.float32), shift_one).astype(
        jnp.bfloat16
    )
    mixed = jnp.dot(hidden_first, proj_qkv, preferred_element_type=jnp.float32)
    bias_pair = bias_qv.astype(jnp.float32)
    queries = (mixed[:, :D] + bias_pair[:D]).astype(jnp.bfloat16)
    keys_own = mixed[:, D : 2 * D].astype(jnp.bfloat16)
    values_own = (mixed[:, 2 * D :] + bias_pair[D:]).astype(jnp.bfloat16)
    keys_all, values_all = (
        lax.all_gather(keys_own, "ctx", axis=0, tiled=True),
        lax.all_gather(values_own, "ctx", axis=0, tiled=True),
    )
    query_heads = queries.reshape(tokens, H, HD)
    key_blocks = keys_all.reshape(block_count, block_rows, H, HD)
    value_blocks = values_all.reshape(block_count, block_rows, H, HD)

    def max_step(state_pair, element):
        key_block, block_start = element
        scores, allowed = masked_scores(
            query_heads, query_pos, key_block, block_start + local_rows, prefix_len
        )
        row_max = jnp.maximum(state_pair[0], jnp.max(scores, axis=-1))
        terms = jnp.where(allowed[None], jnp.exp(scores - row_max[:, :, None]), 0.0)
        row_total = state_pair[1] * jnp.exp(state_pair[0] - row_max) + jnp.sum(terms, axis=-1)
        return ((row_max, row_total), None)

    start_state = (
        jnp.full((H, tokens), NEGATIVE, jnp.float32),
        jnp.zeros((H, tokens), jnp.float32),
    )
    (row_max, row_total), unused = lax.scan(max_step, start_state, (key_blocks, block_starts))
    log_total = row_max + jnp.log(row_total)

    def value_step(attended_sum, element):
        key_block, block_start, value_block = element
        weights_soft = softmax_rows(
            query_heads, query_pos, key_block, block_start + local_rows, prefix_len, log_total
        ).astype(jnp.bfloat16)
        return (
            attended_sum
            + jnp.einsum(
                "hqk,khd->qhd", weights_soft, value_block, preferred_element_type=jnp.float32
            ),
            None,
        )

    attended, unused = lax.scan(
        value_step,
        jnp.zeros((tokens, H, HD), jnp.float32),
        (key_blocks, block_starts, value_blocks),
    )
    attended_low = attended.reshape(tokens, D).astype(jnp.bfloat16)
    branch_one = jnp.dot(
        attended_low, proj_out, preferred_element_type=jnp.float32
    ) + bias_out.astype(jnp.float32)
    resid = inputs + branch_one
    hidden_second = layer_norm(resid, gain_second.astype(jnp.float32), shift_two).astype(
        jnp.bfloat16
    )
    pre_act = jnp.dot(hidden_second, proj_up, preferred_element_type=jnp.float32) + bias_up.astype(
        jnp.float32
    )
    activ = gelu_tanh(pre_act).astype(jnp.bfloat16)
    branch_two = jnp.dot(activ, proj_down, preferred_element_type=jnp.float32) + bias_down.astype(
        jnp.float32
    )
    layer_out = (resid + branch_two).astype(jnp.bfloat16)
    gain_first, proj_qkv, proj_out, gain_second, proj_up, proj_down = (
        lax.all_gather(ln1_gain, ("dp", "ctx"), axis=0, tiled=True),
        lax.all_gather(w_qkv, ("dp", "ctx"), axis=0, tiled=True),
        lax.all_gather(w_out, ("dp", "ctx"), axis=0, tiled=True),
        lax.all_gather(ln2_gain, ("dp", "ctx"), axis=0, tiled=True),
        lax.all_gather(w_up, ("dp", "ctx"), axis=0, tiled=True),
        lax.all_gather(w_down, ("dp", "ctx"), axis=0, tiled=True),
    )
    grad_branch_two = upstream.astype(jnp.bfloat16)
    grad_proj_down = jnp.einsum(
        "tf,td->fd", activ, grad_branch_two, preferred_element_type=jnp.float32
    )
    grad_bias_down = jnp.sum(grad_branch_two.astype(jnp.float32), axis=0)
    grad_activ = jnp.einsum(
        "td,fd->tf", grad_branch_two, proj_down, preferred_element_type=jnp.float32
    )
    gelu_value, gelu_pull = jax.vjp(gelu_tanh, pre_act)
    grad_pre = gelu_pull(grad_activ)[0].astype(jnp.bfloat16)
    grad_proj_up = jnp.einsum(
        "td,tf->df", hidden_second, grad_pre, preferred_element_type=jnp.float32
    )
    grad_bias_up = jnp.sum(grad_pre.astype(jnp.float32), axis=0)
    grad_hidden_second = jnp.einsum(
        "tf,df->td", grad_pre, proj_up, preferred_element_type=jnp.float32
    )
    norm_value, norm_pull = jax.vjp(layer_norm, resid, gain_second.astype(jnp.float32), shift_two)
    resid_part, grad_gain_second, grad_shift_second = norm_pull(grad_hidden_second)
    grad_resid = upstream + resid_part
    grad_branch_one = grad_resid.astype(jnp.bfloat16)
    grad_proj_out = jnp.einsum(
        "td,te->de", attended_low, grad_branch_one, preferred_element_type=jnp.float32
    )
    grad_bias_out = jnp.sum(grad_branch_one.astype(jnp.float32), axis=0)
    grad_attended = jnp.einsum(
        "te,de->td", grad_branch_one, proj_out, preferred_element_type=jnp.float32
    ).astype(jnp.bfloat16)
    grad_heads = grad_attended.reshape(tokens, H, HD)
    row_delta = jnp.sum(grad_heads.astype(jnp.float32) * attended, axis=-1).T

    def back_step(query_sum, element):
        key_block, block_start, value_block = element
        weights_soft = softmax_rows(
            query_heads, query_pos, key_block, block_start + local_rows, prefix_len, log_total
        )
        value_grad = jnp.einsum(
            "hqk,qhd->khd",
            weights_soft.astype(jnp.bfloat16),
            grad_heads,
            preferred_element_type=jnp.float32,
        )
        weight_grad = jnp.einsum(
            "qhd,khd->hqk", grad_heads, value_block, preferred_element_type=jnp.float32
        )
        score_grad = (weights_soft * (weight_grad - row_delta[:, :, None])).astype(jnp.bfloat16)
        query_sum = (
            query_sum
            + jnp.einsum("hqk,khd->qhd", score_grad, key_block, preferred_element_type=jnp.float32)
            * 0.125
        )
        key_grad = (
            jnp.einsum("hqk,qhd->khd", score_grad, query_heads, preferred_element_type=jnp.float32)
            * 0.125
        )
        return (query_sum, (key_grad.reshape(block_rows, D), value_grad.reshape(block_rows, D)))

    query_sum, (key_terms, value_terms) = lax.scan(
        back_step, jnp.zeros((tokens, H, HD), jnp.float32), (key_blocks, block_starts, value_blocks)
    )
    key_sum, value_sum = (
        lax.psum_scatter(
            key_terms.reshape(length, D).astype(jnp.bfloat16),
            "ctx",
            scatter_dimension=0,
            tiled=True,
        ).astype(jnp.float32),
        lax.psum_scatter(
            value_terms.reshape(length, D).astype(jnp.bfloat16),
            "ctx",
            scatter_dimension=0,
            tiled=True,
        ).astype(jnp.float32),
    )
    query_low = query_sum.reshape(tokens, D).astype(jnp.bfloat16)
    key_low = key_sum.astype(jnp.bfloat16)
    value_low = value_sum.astype(jnp.bfloat16)
    grad_qkv = jnp.concatenate([query_low, key_low, value_low], axis=1)
    grad_proj_qkv = jnp.einsum(
        "td,te->de", hidden_first, grad_qkv, preferred_element_type=jnp.float32
    )
    grad_bias_qv = jnp.concatenate(
        [
            jnp.sum(query_low.astype(jnp.float32), axis=0),
            jnp.sum(value_low.astype(jnp.float32), axis=0),
        ]
    )
    grad_hidden_first = jnp.einsum(
        "te,de->td", grad_qkv, proj_qkv, preferred_element_type=jnp.float32
    )
    first_value, first_pull = jax.vjp(layer_norm, inputs, gain_first.astype(jnp.float32), shift_one)
    input_part, grad_gain_first, grad_shift_first = first_pull(grad_hidden_first)
    input_grad = grad_resid + input_part
    (
        sum_gain_first,
        sum_shift_first,
        sum_qkv,
        sum_bias_qv,
        sum_out,
        sum_bias_out,
        sum_gain_second,
        sum_shift_second,
        sum_up,
        sum_bias_up,
        sum_down,
        sum_bias_down,
    ) = (
        lax.psum_scatter(grad_gain_first, ("dp", "ctx"), scatter_dimension=0, tiled=True),
        lax.psum_scatter(grad_shift_first, ("dp", "ctx"), scatter_dimension=0, tiled=True),
        lax.psum_scatter(grad_proj_qkv, ("dp", "ctx"), scatter_dimension=0, tiled=True),
        lax.psum_scatter(grad_bias_qv, ("dp", "ctx"), scatter_dimension=0, tiled=True),
        lax.psum_scatter(grad_proj_out, ("dp", "ctx"), scatter_dimension=0, tiled=True),
        lax.psum_scatter(grad_bias_out, ("dp", "ctx"), scatter_dimension=0, tiled=True),
        lax.psum_scatter(grad_gain_second, ("dp", "ctx"), scatter_dimension=0, tiled=True),
        lax.psum_scatter(grad_shift_second, ("dp", "ctx"), scatter_dimension=0, tiled=True),
        lax.psum_scatter(grad_proj_up, ("dp", "ctx"), scatter_dimension=0, tiled=True),
        lax.psum_scatter(grad_bias_up, ("dp", "ctx"), scatter_dimension=0, tiled=True),
        lax.psum_scatter(grad_proj_down, ("dp", "ctx"), scatter_dimension=0, tiled=True),
        lax.psum_scatter(grad_bias_down, ("dp", "ctx"), scatter_dimension=0, tiled=True),
    )
    return (
        layer_out[None],
        input_grad[None],
        sum_gain_first,
        sum_shift_first,
        sum_qkv,
        sum_bias_qv,
        sum_out,
        sum_bias_out,
        sum_gain_second,
        sum_shift_second,
        sum_up,
        sum_bias_up,
        sum_down,
        sum_bias_down,
    )


def solution(mesh):
    placed = (
        P("dp", "ctx", None),
        P("dp"),
        P(("dp", "ctx")),
        P(("dp", "ctx")),
        P(("dp", "ctx"), None),
        P(("dp", "ctx")),
        P(("dp", "ctx"), None),
        P(("dp", "ctx")),
        P(("dp", "ctx")),
        P(("dp", "ctx")),
        P(("dp", "ctx"), None),
        P(("dp", "ctx")),
        P(("dp", "ctx"), None),
        P(("dp", "ctx")),
        P("dp", "ctx", None),
    )
    return jax.shard_map(
        per_device,
        mesh=mesh,
        in_specs=placed,
        out_specs=(
            P("dp", "ctx", None),
            P("dp", "ctx", None),
            P(("dp", "ctx")),
            P(("dp", "ctx")),
            P(("dp", "ctx"), None),
            P(("dp", "ctx")),
            P(("dp", "ctx"), None),
            P(("dp", "ctx")),
            P(("dp", "ctx")),
            P(("dp", "ctx")),
            P(("dp", "ctx"), None),
            P(("dp", "ctx")),
            P(("dp", "ctx"), None),
            P(("dp", "ctx")),
        ),
        check_vma=False,
    )
```

profile of v0, /device:TPU:0, one launch (start us, length us, event | category | flops | bytes accessed | tf_op | source)
XLA Modules:
  0.0 1624.3 jit_solution(12898448946622320328)
XLA Ops:
  13.8 42.5 %all-reduce.16 = (bf16[1024]{0:T(1024)(128)(2,1)S(1)}, bf16[1024]{0:T(1024)(128)(2,1)S(1)}, bf16[2048]{0:T(1024)(128)(2,1)S(1)}, bf16[1024]{0:T(1024)(128)(2,1)S...) all-reduce(bf16[1024]{0:T(1024)(128)(2,1)S(1)} %dynamic-update-slic, ...), channel_id=1, replica_groups=mesh['dp'=8,'ctx'=4] {'dp','ctx'}, use_global_device_ids=true, to_apply=%add.1 | all-reduce | flops 8192 | bytes 32768
  59.5 23.9 %all-gather.8.cloned.1.call-done = bf16[1024,3072]{1,0:T(8,128)(2,1)} async-done(((bf16[32,3072]{1,0:T(8,128)(2,1)}), bf16[1024,3072]{1,0:T(8,128)(2,1)}) %all-gather.8.cloned.1.call-update) | async-done | bytes 6291472 | tf_op jit(solution)/shard_map/all_gather | solution.py:70
  83.4 4.9 fusion.106
  92.4 66.4 %all-gather = bf16[32,1,128]{2,1,0:T(2,128)(2,1)S(1)} all-gather(bf16[1,1,128]{2,1,0:T(2,128)(2,1)S(1)} %bitcast.227), channel_id=1, replica_groups=mesh['dp'=8,'ctx'=4] {'dp','ctx'}, dimensions={0}, use_global_device_ids=true | all-gather | bytes 8448 | tf_op jit(solution)/shard_map/all_gather | solution.py:77
  160.1 6.4 reshape.292
  166.6 5.4 copy.81
  172.0 9.4 all-gather.12.cloned.1.call-done
  181.4 6.4 reshape.293
  187.8 4.5 copy.82
  192.3 24.0 %while.39 = (s32[]{:T(128)}, f32[16,256]{1,0:T(8,128)S(1)}, f32[16,256]{1,0:T(8,128)S(1)}, s32[2]{0:T(128)S(1)}, s32[]{:T(128)}, /*index=5*/bf16[2,512,16,64]{1,...) while((s32[]{:T(128)}, f32[16,256]{1,0:T(8,128)S(1)}, ...), condition=%wide.region_5.6_spmd.clone, body=%wide.region_2.5_spmd.clone.sunk | while | flops 285497088 | bytes 18963608 | solution.py:123
  195.1 4.7 fusion.161
  199.8 4.5 select_reduce_fusion.2
  207.1 4.7 fusion.161
  211.8 4.5 select_reduce_fusion.2
  216.3 16.0 while.40
  219.1 5.0 fusion.167
  226.9 5.4 fusion.167
  234.4 5.0 all-gather.14.cloned.1.call-done
  243.3 75.1 %all-gather.16.cloned.1.call-done = bf16[1024,4096]{1,0:T(8,128)(2,1)} async-done(((bf16[32,4096]{1,0:T(8,128)(2,1)}), bf16[1024,4096]{1,0:T(8,128)(2,1)}) %all-gather.16.cloned.1.call-update) | async-done | bytes 8388624 | tf_op jit(solution)/shard_map/all_gather | solution.py:76
  318.5 8.2 convolution_add_fusion
  326.7 70.6 %all-gather.18.cloned.1.call-done = bf16[4096,1024]{1,0:T(8,128)(2,1)} async-done(((bf16[128,1024]{1,0:T(8,128)(2,1)}), bf16[4096,1024]{1,0:T(8,128)(2,1)}) %all-gather.18.cloned.1.call-update) | async-done | bytes 8388624 | tf_op jit(solution)/shard_map/all_gather | solution.py:78
  397.3 8.7 convert_reduce_fusion
  407.3 3.2 multiply_reduce_fusion
  418.6 63.5 %while.41 = (s32[]{:T(128)}, f32[256,16,64]{0,2,1:T(8,128)}, bf16[2,512,1024]{2,1,0:T(8,128)(2,1)}, bf16[2,512,1024]{2,1,0:T(8,128)(2,1)}, bf16[2,512,16,64]{1,3...) while((s32[]{:T(128)}, f32[256,16,64]{0,2,1:T(8,128)}, ...), condition=%wide.region_14.15_spmd.clone, body=%wide.region_13.14_spmd.clone.sunk | while | flops 1369442048 | bytes 102161728 | solution.py:225
  422.9 4.5 fusion.179
  427.4 4.0 fusion.180
  431.5 6.5 fusion.181
  440.3 4.5 convolution_multiply_fusion.3
  447.1 3.0 constant_dynamic-update-slice_fusion.3
  454.5 4.5 fusion.179
  459.0 4.3 fusion.180
  463.3 6.5 fusion.181
  472.1 4.5 convolution_multiply_fusion.3
  478.9 3.1 constant_dynamic-update-slice_fusion.3
  482.0 4.1 copy.89
  488.9 3.7 fusion.115
  494.0 34.7 %reduce-scatter.9.cloned.1.call-done = bf16[256,1024]{0,1:T(8,128)(2,1)} async-done(((bf16[1024,1024]{0,1:T(8,128)(2,1)}), bf16[256,1024]{0,1:T(8,128)(2,1)}) %reduce-scatter.9.cloned.1.call-update) | async-done | bytes 524304 | tf_op jit(solution)/shard_map/reduce_scatter | solution.py:235
  528.8 45.6 %reduce-scatter.7.cloned.1.call-done = bf16[256,1024]{0,1:T(8,128)(2,1)} async-done(((bf16[1024,1024]{0,1:T(8,128)(2,1)}), bf16[256,1024]{0,1:T(8,128)(2,1)}) %reduce-scatter.7.cloned.1.call-update) | async-done | bytes 524304 | tf_op jit(solution)/shard_map/reduce_scatter | solution.py:229
  574.4 7.7 fusion.93
  583.4 9.8 fusion.109
  594.3 10.7 fusion.95
  605.7 8.3 fusion.82
  614.4 4.9 fusion.110
  621.4 41.1 %all-reduce.15 = (f32[1024]{0:T(1024)S(1)}, f32[1024]{0:T(1024)S(1)}, f32[2048]{0:T(1024)S(1)}, f32[1024]{0:T(1024)S(1)}, f32[1024]{0:T(1024)S(1)}, /*index=5*/f...) all-reduce(f32[1024]{0:T(1024)S(1)} %get-tuple-element.430, ...), channel_id=4, replica_groups=mesh['dp'=8,'ctx'=4] {'dp','ctx'}, use_global_device_ids=true, to_apply=%region_20.21.clone | all-reduce | flops 12288 | bytes 98304
  667.1 58.2 %reduce-scatter.13.cloned.1.call-done = f32[32,1024]{1,0:T(8,128)} async-done(((f32[1024,1024]{1,0:T(8,128)}), f32[32,1024]{1,0:T(8,128)}) %reduce-scatter.13.cloned.1.call-update) | async-done | bytes 131088 | tf_op jit(solution)/shard_map/reduce_scatter | solution.py:279
  725.3 160.5 %reduce-scatter.11.cloned.1.call-done = f32[32,3072]{1,0:T(8,128)} async-done(((f32[1024,3072]{1,0:T(8,128)}), f32[32,3072]{1,0:T(8,128)}) %reduce-scatter.11.cloned.1.call-update) | async-done | bytes 393232 | tf_op jit(solution)/shard_map/reduce_scatter | solution.py:277
  885.8 366.4 %reduce-scatter.15.cloned.1.call-done = f32[32,4096]{1,0:T(8,128)} async-done(((f32[1024,4096]{1,0:T(8,128)}), f32[32,4096]{1,0:T(8,128)}) %reduce-scatter.15.cloned.1.call-update) | async-done | bytes 524304 | tf_op jit(solution)/shard_map/reduce_scatter | solution.py:283
  1252.2 365.0 %reduce-scatter.17.cloned.1.call-done = f32[128,1024]{1,0:T(8,128)} async-done(((f32[4096,1024]{1,0:T(8,128)}), f32[128,1024]{1,0:T(8,128)}) %reduce-scatter.17.cloned.1.call-update) | async-done | bytes 524304 | tf_op jit(solution)/shard_map/reduce_scatter | solution.py:285
  (223 shorter events, 73.1 us)
Async XLA Ops:
  7.2 76.2 %all-gather.8.cloned.1.call-start = ((), (), s32[]{:S(2)}) async-start(), calls=%async_computation.6 | async-start | bytes 6488064 | tf_op jit(solution)/shard_map/all_gather | solution.py:70
  7.9 152.2 %all-gather.10.cloned.1.call-start = ((), (), s32[]{:S(2)}) async-start(), calls=%async_computation.7 | async-start | bytes 2621440 | tf_op jit(solution)/shard_map/all_gather | solution.py:103
  56.4 31.9 %copy-start.24 = (f32[1024]{0:T(1024)}, f32[1024]{0:T(1024)S(1)}, u32[]{:S(2)}) copy-start(f32[1024]{0:T(1024)S(1)} %convert_element_type.122) | copy-start | bytes 12292
  56.4 31.9 %copy-start.22 = (f32[1024]{0:T(1024)}, f32[1024]{0:T(1024)S(1)}, u32[]{:S(2)}) copy-start(f32[1024]{0:T(1024)S(1)} %convert_element_type.121) | copy-start | bytes 12292
  57.6 30.7 %copy-start.26 = (f32[256]{0:T(256)}, f32[256]{0:T(256)S(1)}, u32[]{:S(2)}) copy-start(f32[256]{0:T(256)S(1)} %broadcast_multiply_fusion.1) | copy-start | bytes 3076
  58.9 29.3 %copy-start.28 = (f32[256]{0:T(256)}, f32[256]{0:T(256)S(1)}, u32[]{:S(2)}) copy-start(f32[256]{0:T(256)S(1)} %fusion.101) | copy-start | bytes 3076
  88.3 4.1 copy-start.39
  89.5 91.8 %all-gather.12.cloned.1.call-start = ((), (), s32[]{:S(2)}) async-start(), calls=%async_computation.8 | async-start | bytes 2621440 | tf_op jit(solution)/shard_map/all_gather | solution.py:102
  90.5 148.9 %all-gather.14.cloned.1.call-start = ((), (), s32[]{:S(2)}) async-start(), calls=%async_computation.9 | async-start | bytes 2162688 | tf_op jit(solution)/shard_map/all_gather | solution.py:72
  91.1 227.4 %all-gather.16.cloned.1.call-start = ((), (), s32[]{:S(2)}) async-start(), calls=%async_computation.10 | async-start | bytes 8650752 | tf_op jit(solution)/shard_map/all_gather | solution.py:76
  91.7 305.6 %all-gather.18.cloned.1.call-start = ((), (), s32[]{:S(2)}) async-start(), calls=%async_computation.11 | async-start | bytes 8650752 | tf_op jit(solution)/shard_map/all_gather | solution.py:78
  92.2 436.5 %reduce-scatter.9.cloned.1.call-start = ((), (), s32[]{:S(2)}) async-start(), calls=%async_computation.13 | async-start | bytes 2621440 | tf_op jit(solution)/shard_map/reduce_scatter | solution.py:235
  216.3 23.1 %copy-start.2 = (bf16[1,256,1024]{2,1,0:T(8,128)(2,1)S(1)}, bf16[1,256,1024]{2,1,0:T(8,128)(2,1)}, u32[]{:S(2)}) copy-start(bf16[1,256,1024]{2,1,0:T(8,128)(2,1)} %param.21) | copy-start | bytes 1572868
  397.3 10.0 copy-start.4
  397.3 10.0 copy-start.40
  407.3 4.6 copy-start.9
  410.4 3.0 copy-start.14
  410.9 4.2 copy-start.34
  418.6 4.3 copy-start.11
  418.6 4.3 copy-start.16
  419.9 7.5 copy-start
  427.4 4.0 copy-start.17
  450.1 4.3 copy-start.11
  450.1 4.3 copy-start.16
  451.5 7.5 copy-start
  459.0 4.3 copy-start.17
  482.0 4.2 copy-start.18
  486.1 2.7 copy-start.8
  486.1 88.2 %reduce-scatter.7.cloned.1.call-start = ((), (), s32[]{:S(2)}) async-start(), calls=%async_computation.12 | async-start | bytes 2621440 | tf_op jit(solution)/shard_map/reduce_scatter | solution.py:229
  488.8 236.5 %reduce-scatter.13.cloned.1.call-start = ((), (), s32[]{:S(2)}) async-start(), calls=%async_computation.15 | async-start | bytes 4325376 | tf_op jit(solution)/shard_map/reduce_scatter | solution.py:279
  492.6 81.8 %copy-start.23 = (f32[1024]{0:T(1024)S(1)}, f32[1024]{0:T(1024)}, u32[]{:S(2)}) copy-start(f32[1024]{0:T(1024)} %copy-done.22) | copy-start | bytes 12292
  492.6 81.8 %copy-start.25 = (f32[1024]{0:T(1024)S(1)}, f32[1024]{0:T(1024)}, u32[]{:S(2)}) copy-start(f32[1024]{0:T(1024)} %copy-done.24) | copy-start | bytes 12292
  492.6 81.8 %copy-start.27 = (f32[256]{0:T(256)S(1)}, f32[256]{0:T(256)}, u32[]{:S(2)}) copy-start(f32[256]{0:T(256)} %copy-done.26) | copy-start | bytes 3076
  492.6 81.8 %copy-start.29 = (f32[256]{0:T(256)S(1)}, f32[256]{0:T(256)}, u32[]{:S(2)}) copy-start(f32[256]{0:T(256)} %copy-done.28) | copy-start | bytes 3076
  492.6 393.2 %reduce-scatter.11.cloned.1.call-start = ((), (), s32[]{:S(2)}) async-start(), calls=%async_computation.14 | async-start | bytes 12976128 | tf_op jit(solution)/shard_map/reduce_scatter | solution.py:277
  494.0 88.1 %copy-start.12 = (bf16[256,16,64]{0,2,1:T(8,128)(2,1)}, bf16[256,16,64]{0,2,1:T(8,128)(2,1)S(1)}, u32[]{:S(2)}) copy-start(bf16[256,16,64]{0,2,1:T(8,128)(2,1)S(1)} %get-tuple-element.513) | copy-start | bytes 1572868
  582.2 670.0 %reduce-scatter.15.cloned.1.call-start = ((), (), s32[]{:S(2)}) async-start(), calls=%async_computation.16 | async-start | bytes 17301504 | tf_op jit(solution)/shard_map/reduce_scatter | solution.py:283
  593.2 1024.0 %reduce-scatter.17.cloned.1.call-start = ((), (), s32[]{:S(2)}) async-start(), calls=%async_computation.17 | async-start | bytes 17301504 | tf_op jit(solution)/shard_map/reduce_scatter | solution.py:285
  605.7 8.4 copy-start.15
  605.7 8.6 copy-start.13
  605.7 8.6 copy-start.21
  614.3 5.0 copy-start.33
  614.3 5.5 copy-start.7
  614.3 5.5 copy-start.35
  619.3 2.1 copy-start.30
  619.3 2.1 copy-start.31
  619.3 2.1 copy-start.36
  619.3 2.1 copy-start.37
  (9 other events, 9.0 us)
Sparse Core Ops, SparseCore 0:
  10.9 72.4 all-gather.7
  89.7 44.5 all-gather.9
  136.4 44.8 all-gather.11
  184.2 55.2 all-gather.13
  242.2 76.2 all-gather.15
  321.2 75.9 all-gather.17
  486.3 42.4 reduce-scatter.8
  531.1 43.1 reduce-scatter.6
  577.2 148.0 reduce-scatter.12
  731.8 153.9 reduce-scatter.10
  888.8 363.3 reduce-scatter.14
  1255.0 362.1 reduce-scatter.16
where the time goes:
time: 1630 us; the launch traced here: 1620 us
  waiting for transfers between devices  1220 us (75%)
  blocking collectives  150 us (9%)
  matrix products  136 us (8%)
  local copies, waits for them, and re-layouts  71.7 us (4%)
  other arithmetic  33.5 us (2%)
    reduce_scatter x1, waiting for transfers between devices, per_device(): lax.psum_scatter(grad_proj_up, ('dp', 'ctx'), scatter_dimension=0, tiled=...  366 us
    reduce_scatter x1, waiting for transfers between devices, per_device(): lax.psum_scatter(grad_proj_down, ('dp', 'ctx'), scatter_dimension=0, tile...  365 us
    reduce_scatter x1, waiting for transfers between devices, per_device(): lax.psum_scatter(grad_proj_qkv, ('dp', 'ctx'), scatter_dimension=0, tiled...  160 us
    unnamed x2, blocking collectives  83.6 us
    all_gather x1, waiting for transfers between devices, per_device(): lax.all_gather(w_up, ('dp', 'ctx'), axis=0, tiled=True)  75.1 us
    all_gather x1, waiting for transfers between devices, per_device(): lax.all_gather(w_down, ('dp', 'ctx'), axis=0, tiled=True)  70.6 us
    all_gather x1, blocking collectives, per_device(): lax.all_gather(b_up, ('dp', 'ctx'), axis=0, tiled=True)  66.4 us
    reduce_scatter x1, waiting for transfers between devices, per_device(): lax.psum_scatter(grad_proj_out, ('dp', 'ctx'), scatter_dimension=0, tiled...  58.2 us
  transfers between devices with their start and end apart: 12, of which 11 were waited for; matrix products, arithmetic and copies ran while one was open for 9% of the time, Pallas kernels for 0%

commit v1 on v0

--- a/solution.py
+++ b/solution.py
@@ -7,6 +7,27 @@
 H = 16
 HD = 64
 NEGATIVE = -1e30
+
+
+def laid_out(pieces, dim):
+    pieces = jnp.moveaxis(pieces, 0, dim)
+    dims = pieces.shape
+    return pieces.reshape(*dims[:dim], dims[dim] * dims[dim + 1], *dims[dim + 2 :])
+
+
+def grow_blocks(shard, axis):
+    size, position = (lax.axis_size(axis), lax.axis_index(axis))
+    blocks, bit = (shard[None], 1)
+    while bit < size:
+        other = lax.ppermute(blocks, axis, [(i, i ^ bit) for i in range(size)])
+        low = position & bit == 0
+        blocks = jnp.concatenate([jnp.where(low, blocks, other), jnp.where(low, other, blocks)])
+        bit *= 2
+    return blocks
+
+
+def gather_by_bits(x, axis, dim):
+    return laid_out(grow_blocks(x, axis), dim)
 
 
 def layer_norm(values, gain, shift):
@@ -74,7 +95,7 @@
         lax.all_gather(ln2_gain, ("dp", "ctx"), axis=0, tiled=True),
         lax.all_gather(ln2_bias, ("dp", "ctx"), axis=0, tiled=True),
         lax.all_gather(w_up, ("dp", "ctx"), axis=0, tiled=True),
-        lax.all_gather(b_up, ("dp", "ctx"), axis=0, tiled=True),
+        gather_by_bits(b_up, ("dp", "ctx"), 0),
         lax.all_gather(w_down, ("dp", "ctx"), axis=0, tiled=True),
         lax.all_gather(b_down, ("dp", "ctx"), axis=0, tiled=True),
     )

time: 1630 us -> 1630 us (level)
  blocking collectives: 150 us -> 83.5 us
  waiting for transfers between devices: 1220 us -> 1270 us
    all_gather x1 -> x0, blocking collectives: 66.4 us -> none  [per_device(): lax.all_gather(b_up, ('dp', 'ctx'), axis=0, tiled=True)]
    all_gather x1, waiting for transfers between devices: 9.36 us -> 34.4 us  [per_device(): lax.all_gather(keys_own, 'ctx', axis=0, tiled=True)]
    all_gather x1, waiting for transfers between devices: 0.02 us -> 23.8 us  [per_device(): lax.all_gather(values_own, 'ctx', axis=0, tiled=True)]
  transfers between devices with their start and end apart: 12 -> 17, of which waited for: 11 -> 17; matrix products, arithmetic and copies ran while one was open for 9% -> 9% of each run, Pallas kernels for 0% -> 0%
where the time goes in v1:
time: 1630 us; the launch traced here: 1620 us
  waiting for transfers between devices  1270 us (78%)
  matrix products  136 us (8%)
  blocking collectives  83.5 us (5%)
  local copies, waits for them, and re-layouts  72.3 us (4%)
  other arithmetic  33.6 us (2%)
    reduce_scatter x1, waiting for transfers between devices, per_device(): lax.psum_scatter(grad_proj_up, ('dp', 'ctx'), scatter_dimension=0, tiled=...  366 us
    reduce_scatter x1, waiting for transfers between devices, per_device(): lax.psum_scatter(grad_proj_down, ('dp', 'ctx'), scatter_dimension=0, tile...  365 us
    reduce_scatter x1, waiting for transfers between devices, per_device(): lax.psum_scatter(grad_proj_qkv, ('dp', 'ctx'), scatter_dimension=0, tiled...  160 us
    unnamed x2, blocking collectives  83.5 us
    all_gather x1, waiting for transfers between devices, per_device(): lax.all_gather(w_up, ('dp', 'ctx'), axis=0, tiled=True)  75.2 us
    all_gather x1, waiting for transfers between devices, per_device(): lax.all_gather(w_down, ('dp', 'ctx'), axis=0, tiled=True)  70.6 us
    reduce_scatter x1, waiting for transfers between devices, per_device(): lax.psum_scatter(grad_proj_out, ('dp', 'ctx'), scatter_dimension=0, tiled...  58.2 us
    reduce_scatter x1, waiting for transfers between devices, per_device(): lax.psum_scatter(key_terms.reshape(length, D).astype(jnp.bfloat16), 'ctx'...  45.6 us
  transfers between devices with their start and end apart: 17, of which 17 were waited for; matrix products, arithmetic and copies ran while one was open for 9% of the time, Pallas kernels for 0%

profile of v1, /device:TPU:0, one launch (start us, length us, event | category | flops | bytes accessed | tf_op | source)
XLA Modules:
  0.0 1623.2 jit_solution(14842329164817118260)
XLA Ops:
  13.8 42.5 %all-reduce.16 = (bf16[1024]{0:T(1024)(128)(2,1)S(1)}, bf16[1024]{0:T(1024)(128)(2,1)S(1)}, bf16[2048]{0:T(1024)(128)(2,1)S(1)}, bf16[1024]{0:T(1024)(128)(2,1)S...) all-reduce(bf16[1024]{0:T(1024)(128)(2,1)S(1)} %dynamic-update-slic, ...), channel_id=1, replica_groups=mesh['dp'=8,'ctx'=4] {'dp','ctx'}, use_global_device_ids=true, to_apply=%add.1 | all-reduce | flops 8192 | bytes 32768
  59.5 23.9 %all-gather.7.cloned.1.call-done = bf16[1024,3072]{1,0:T(8,128)(2,1)} async-done(((bf16[32,3072]{1,0:T(8,128)(2,1)}), bf16[1024,3072]{1,0:T(8,128)(2,1)}) %all-gather.7.cloned.1.call-update) | async-done | bytes 6291472 | tf_op jit(solution)/shard_map/all_gather | solution.py:91
  83.4 4.9 fusion.107
  110.4 23.8 %all-gather.9.cloned.1.call-done = bf16[1024,1024]{1,0:T(8,128)(2,1)} async-done(((bf16[256,1024]{1,0:T(8,128)(2,1)}), bf16[1024,1024]{1,0:T(8,128)(2,1)}) %all-gather.9.cloned.1.call-update) | async-done | bytes 2097168 | tf_op jit(solution)/shard_map/all_gather | solution.py:124
  134.2 6.9 reshape.297
  141.1 5.5 copy.81
  146.6 34.4 %all-gather.11.cloned.1.call-done = bf16[1024,1024]{1,0:T(8,128)(2,1)} async-done(((bf16[256,1024]{1,0:T(8,128)(2,1)}), bf16[1024,1024]{1,0:T(8,128)(2,1)}) %all-gather.11.cloned.1.call-update) | async-done | bytes 2097168 | tf_op jit(solution)/shard_map/all_gather | solution.py:123
  181.0 6.5 reshape.298
  187.4 4.5 copy.82
  191.9 24.0 %while.39 = (s32[]{:T(128)}, f32[16,256]{1,0:T(8,128)S(1)}, f32[16,256]{1,0:T(8,128)S(1)}, s32[2]{0:T(128)S(1)}, s32[]{:T(128)}, /*index=5*/bf16[2,512,16,64]{1,...) while((s32[]{:T(128)}, f32[16,256]{1,0:T(8,128)S(1)}, ...), condition=%wide.region_5.6_spmd.clone, body=%wide.region_2.5_spmd.clone.sunk | while | flops 285497088 | bytes 18963608 | solution.py:144
  194.7 4.7 fusion.162
  199.4 4.5 select_reduce_fusion.2
  206.7 4.7 fusion.162
  211.4 4.5 select_reduce_fusion.2
  216.0 16.0 while.40
  218.8 5.0 fusion.168
  226.6 5.4 fusion.168
  234.0 5.0 all-gather.13.cloned.1.call-done
  242.9 75.2 %all-gather.15.cloned.1.call-done = bf16[1024,4096]{1,0:T(8,128)(2,1)} async-done(((bf16[32,4096]{1,0:T(8,128)(2,1)}), bf16[1024,4096]{1,0:T(8,128)(2,1)}) %all-gather.15.cloned.1.call-update) | async-done | bytes 8388624 | tf_op jit(solution)/shard_map/all_gather | solution.py:97
  318.1 8.2 convolution_add_fusion
  326.3 70.6 %all-gather.17.cloned.1.call-done = bf16[4096,1024]{1,0:T(8,128)(2,1)} async-done(((bf16[128,1024]{1,0:T(8,128)(2,1)}), bf16[4096,1024]{1,0:T(8,128)(2,1)}) %all-gather.17.cloned.1.call-update) | async-done | bytes 8388624 | tf_op jit(solution)/shard_map/all_gather | solution.py:99
  396.9 8.7 convert_reduce_fusion
  406.9 3.2 multiply_reduce_fusion
  418.2 63.5 %while.41 = (s32[]{:T(128)}, f32[256,16,64]{0,2,1:T(8,128)}, bf16[2,512,1024]{2,1,0:T(8,128)(2,1)}, bf16[2,512,1024]{2,1,0:T(8,128)(2,1)}, bf16[2,512,16,64]{1,3...) while((s32[]{:T(128)}, f32[256,16,64]{0,2,1:T(8,128)}, ...), condition=%wide.region_14.15_spmd.clone, body=%wide.region_13.14_spmd.clone.sunk | while | flops 1369442048 | bytes 102161728 | solution.py:246
  422.5 4.5 fusion.180
  427.1 4.0 fusion.181
  431.1 6.5 fusion.182
  439.9 4.5 convolution_multiply_fusion.3
  446.7 3.0 constant_dynamic-update-slice_fusion.3
  454.1 4.5 fusion.180
  458.6 4.3 fusion.181
  462.9 6.5 fusion.182
  471.8 4.5 convolution_multiply_fusion.3
  478.6 3.1 constant_dynamic-update-slice_fusion.3
  481.7 4.1 copy.89
  488.5 3.7 fusion.116
  493.7 34.7 %reduce-scatter.9.cloned.1.call-done = bf16[256,1024]{0,1:T(8,128)(2,1)} async-done(((bf16[1024,1024]{0,1:T(8,128)(2,1)}), bf16[256,1024]{0,1:T(8,128)(2,1)}) %reduce-scatter.9.cloned.1.call-update) | async-done | bytes 524304 | tf_op jit(solution)/shard_map/reduce_scatter | solution.py:256
  528.4 45.6 %reduce-scatter.7.cloned.1.call-done = bf16[256,1024]{0,1:T(8,128)(2,1)} async-done(((bf16[1024,1024]{0,1:T(8,128)(2,1)}), bf16[256,1024]{0,1:T(8,128)(2,1)}) %reduce-scatter.7.cloned.1.call-update) | async-done | bytes 524304 | tf_op jit(solution)/shard_map/reduce_scatter | solution.py:250
  574.0 7.7 fusion.93
  583.0 9.8 fusion.110
  593.8 10.7 fusion.95
  605.3 8.3 fusion.82
  613.9 4.9 fusion.111
  621.0 41.0 %all-reduce.15 = (f32[1024]{0:T(1024)S(1)}, f32[1024]{0:T(1024)S(1)}, f32[2048]{0:T(1024)S(1)}, f32[1024]{0:T(1024)S(1)}, f32[1024]{0:T(1024)S(1)}, /*index=5*/f...) all-reduce(f32[1024]{0:T(1024)S(1)} %get-tuple-element.430, ...), channel_id=4, replica_groups=mesh['dp'=8,'ctx'=4] {'dp','ctx'}, use_global_device_ids=true, to_apply=%region_20.21.clone | all-reduce | flops 12288 | bytes 98304
  666.7 58.2 %reduce-scatter.13.cloned.1.call-done = f32[32,1024]{1,0:T(8,128)} async-done(((f32[1024,1024]{1,0:T(8,128)}), f32[32,1024]{1,0:T(8,128)}) %reduce-scatter.13.cloned.1.call-update) | async-done | bytes 131088 | tf_op jit(solution)/shard_map/reduce_scatter | solution.py:300
  724.9 159.9 %reduce-scatter.11.cloned.1.call-done = f32[32,3072]{1,0:T(8,128)} async-done(((f32[1024,3072]{1,0:T(8,128)}), f32[32,3072]{1,0:T(8,128)}) %reduce-scatter.11.cloned.1.call-update) | async-done | bytes 393232 | tf_op jit(solution)/shard_map/reduce_scatter | solution.py:298
  884.8 366.3 %reduce-scatter.15.cloned.1.call-done = f32[32,4096]{1,0:T(8,128)} async-done(((f32[1024,4096]{1,0:T(8,128)}), f32[32,4096]{1,0:T(8,128)}) %reduce-scatter.15.cloned.1.call-update) | async-done | bytes 524304 | tf_op jit(solution)/shard_map/reduce_scatter | solution.py:304
  1251.1 365.0 %reduce-scatter.17.cloned.1.call-done = f32[128,1024]{1,0:T(8,128)} async-done(((f32[4096,1024]{1,0:T(8,128)}), f32[128,1024]{1,0:T(8,128)}) %reduce-scatter.17.cloned.1.call-update) | async-done | bytes 524304 | tf_op jit(solution)/shard_map/reduce_scatter | solution.py:306
  (241 shorter events, 89.9 us)
Async XLA Ops:
  7.2 76.2 %all-gather.7.cloned.1.call-start = ((), (), s32[]{:S(2)}) async-start(), calls=%async_computation.6 | async-start | bytes 6488064 | tf_op jit(solution)/shard_map/all_gather | solution.py:91
  7.9 126.2 %all-gather.9.cloned.1.call-start = ((), (), s32[]{:S(2)}) async-start(), calls=%async_computation.7 | async-start | bytes 2621440 | tf_op jit(solution)/shard_map/all_gather | solution.py:124
  56.4 31.9 %copy-start.24 = (f32[1024]{0:T(1024)}, f32[1024]{0:T(1024)S(1)}, u32[]{:S(2)}) copy-start(f32[1024]{0:T(1024)S(1)} %convert_element_type.129) | copy-start | bytes 12292
  56.4 31.9 %copy-start.22 = (f32[1024]{0:T(1024)}, f32[1024]{0:T(1024)S(1)}, u32[]{:S(2)}) copy-start(f32[1024]{0:T(1024)S(1)} %convert_element_type.128) | copy-start | bytes 12292
  57.6 30.7 %copy-start.26 = (f32[256]{0:T(256)}, f32[256]{0:T(256)S(1)}, u32[]{:S(2)}) copy-start(f32[256]{0:T(256)S(1)} %broadcast_multiply_fusion.1) | copy-start | bytes 3076
  58.9 29.3 %copy-start.28 = (f32[256]{0:T(256)}, f32[256]{0:T(256)S(1)}, u32[]{:S(2)}) copy-start(f32[256]{0:T(256)S(1)} %fusion.102) | copy-start | bytes 3076
  88.3 4.0 copy-start.39
  89.5 91.4 %all-gather.11.cloned.1.call-start = ((), (), s32[]{:S(2)}) async-start(), calls=%async_computation.8 | async-start | bytes 2621440 | tf_op jit(solution)/shard_map/all_gather | solution.py:123
  90.5 148.5 %all-gather.13.cloned.1.call-start = ((), (), s32[]{:S(2)}) async-start(), calls=%async_computation.9 | async-start | bytes 2162688 | tf_op jit(solution)/shard_map/all_gather | solution.py:93
  91.1 227.0 %all-gather.15.cloned.1.call-start = ((), (), s32[]{:S(2)}) async-start(), calls=%async_computation.10 | async-start | bytes 8650752 | tf_op jit(solution)/shard_map/all_gather | solution.py:97
  91.7 305.2 %all-gather.17.cloned.1.call-start = ((), (), s32[]{:S(2)}) async-start(), calls=%async_computation.11 | async-start | bytes 8650752 | tf_op jit(solution)/shard_map/all_gather | solution.py:99
  92.2 436.2 %reduce-scatter.9.cloned.1.call-start = ((), (), s32[]{:S(2)}) async-start(), calls=%async_computation.13 | async-start | bytes 2621440 | tf_op jit(solution)/shard_map/reduce_scatter | solution.py:256
  92.3 3.6 collective-permute-start
  95.9 4.6 collective-permute-start.1
  100.5 1.2 collective-permute-start.2
  101.8 3.7 collective-permute-start.3
  105.5 3.7 collective-permute-start.4
  216.0 23.0 %copy-start.2 = (bf16[1,256,1024]{2,1,0:T(8,128)(2,1)S(1)}, bf16[1,256,1024]{2,1,0:T(8,128)(2,1)}, u32[]{:S(2)}) copy-start(bf16[1,256,1024]{2,1,0:T(8,128)(2,1)} %param.21) | copy-start | bytes 1572868
  396.9 10.0 copy-start.4
  396.9 10.0 copy-start.40
  406.9 4.6 copy-start.9
  410.1 3.0 copy-start.14
  410.5 4.1 copy-start.34
  418.2 4.3 copy-start.11
  418.2 4.3 copy-start.16
  419.5 7.5 copy-start
  427.1 4.0 copy-start.17
  449.8 4.3 copy-start.11
  449.8 4.3 copy-start.16
  451.1 7.5 copy-start
  458.6 4.3 copy-start.17
  481.7 4.2 copy-start.18
  485.8 88.2 %reduce-scatter.7.cloned.1.call-start = ((), (), s32[]{:S(2)}) async-start(), calls=%async_computation.12 | async-start | bytes 2621440 | tf_op jit(solution)/shard_map/reduce_scatter | solution.py:250
  488.5 236.4 %reduce-scatter.13.cloned.1.call-start = ((), (), s32[]{:S(2)}) async-start(), calls=%async_computation.15 | async-start | bytes 4325376 | tf_op jit(solution)/shard_map/reduce_scatter | solution.py:300
  492.2 81.7 %copy-start.23 = (f32[1024]{0:T(1024)S(1)}, f32[1024]{0:T(1024)}, u32[]{:S(2)}) copy-start(f32[1024]{0:T(1024)} %copy-done.22) | copy-start | bytes 12292
  492.2 81.7 %copy-start.25 = (f32[1024]{0:T(1024)S(1)}, f32[1024]{0:T(1024)}, u32[]{:S(2)}) copy-start(f32[1024]{0:T(1024)} %copy-done.24) | copy-start | bytes 12292
  492.2 81.8 %copy-start.27 = (f32[256]{0:T(256)S(1)}, f32[256]{0:T(256)}, u32[]{:S(2)}) copy-start(f32[256]{0:T(256)} %copy-done.26) | copy-start | bytes 3076
  492.3 81.7 %copy-start.29 = (f32[256]{0:T(256)S(1)}, f32[256]{0:T(256)}, u32[]{:S(2)}) copy-start(f32[256]{0:T(256)} %copy-done.28) | copy-start | bytes 3076
  492.3 392.5 %reduce-scatter.11.cloned.1.call-start = ((), (), s32[]{:S(2)}) async-start(), calls=%async_computation.14 | async-start | bytes 12976128 | tf_op jit(solution)/shard_map/reduce_scatter | solution.py:298
  493.7 88.0 %copy-start.12 = (bf16[256,16,64]{0,2,1:T(8,128)(2,1)}, bf16[256,16,64]{0,2,1:T(8,128)(2,1)S(1)}, u32[]{:S(2)}) copy-start(bf16[256,16,64]{0,2,1:T(8,128)(2,1)S(1)} %get-tuple-element.513) | copy-start | bytes 1572868
  581.7 669.3 %reduce-scatter.15.cloned.1.call-start = ((), (), s32[]{:S(2)}) async-start(), calls=%async_computation.16 | async-start | bytes 17301504 | tf_op jit(solution)/shard_map/reduce_scatter | solution.py:304
  592.8 1023.3 %reduce-scatter.17.cloned.1.call-start = ((), (), s32[]{:S(2)}) async-start(), calls=%async_computation.17 | async-start | bytes 17301504 | tf_op jit(solution)/shard_map/reduce_scatter | solution.py:306
  605.3 8.3 copy-start.15
  605.3 8.6 copy-start.13
  605.3 8.6 copy-start.21
  613.9 5.0 copy-start.33
  613.9 5.5 copy-start.7
  613.9 5.5 copy-start.35
  (14 other events, 20.2 us)
Sparse Core Ops, SparseCore 0:
  10.9 72.4 all-gather.6
  89.7 44.4 all-gather.8
  136.3 44.6 all-gather.10
  183.8 55.1 all-gather.12
  241.8 76.2 all-gather.14
  320.9 75.9 all-gather.16
  485.9 42.4 reduce-scatter.8
  530.8 43.1 reduce-scatter.6
  576.8 147.9 reduce-scatter.12
  731.3 153.4 reduce-scatter.10
  887.7 363.2 reduce-scatter.14
  1253.9 362.1 reduce-scatter.16
